TPU v7x, 128 devices: a whole 4x4x4 slice. The times are simulated.
128 devices in a mesh: row: 8 (over y, core), col: 16 (over x, z).
Axes of the slice: x: 4, y: 4, z: 4, core: 2. Of those that a mesh axis runs over, the one named last changes fastest.
Arguments:
- tokens: bfloat16 [104, 320, 384], P('row', 'col')
- row_sizes: int32 [8], replicated, may hold values from 1 to 13, 88 in all
- col_sizes: int32 [16], replicated, may hold values from 1 to 20, 256 in all
- norm_gain: float32 [384], replicated, may hold values from 0.25 to 1.75
- query_weight: bfloat16 [384, 384], replicated
- key_weight: bfloat16 [384, 384], replicated
- value_weight: bfloat16 [384, 384], replicated, may hold values from -0.3125 to 0.3125
- out_weight: bfloat16 [384, 384], replicated, may hold values from -0.625 to 0.625
- cache_one: bfloat16 [2, 104, 320, 384], P(None, 'row', 'col'), may hold values from -6 to 6
- gain_one: float32 [384], replicated, may hold values from 0.25 to 1.75
- conv_one: bfloat16 [3, 3, 3, 384, 384], replicated, may hold values from -0.0625 to 0.0625
- cache_two: bfloat16 [2, 208, 640, 384], P(None, 'row', 'col'), may hold values from -6 to 6
- gain_two: float32 [384], replicated, may hold values from 0.25 to 1.75
- conv_two: bfloat16 [3, 3, 3, 384, 192], replicated, may hold values from -0.0625 to 0.0625
Outputs:
- decoded: bfloat16 [208, 640, 192], P('row', 'col')
Inputs may be any that keep to these rules, and one draw needn't show every extreme that they name: `row_sizes`: positive tile heights that sum to 88; the tallest has exactly 13 rows. `col_sizes`: positive tile widths that sum to 256; the widest has exactly 20 columns.
All inputs are finite; a program needn't handle non-finite values.
Results may differ from a plain program's by a relative error of at most 0.0095.
Values may be sent and summed in bfloat16 or wider, within the bound.
No kernel may reach another device: no remote copies, remote signals or barrier semaphores. Data moves between devices by JAX's collectives and lax.ppermute only.
A program may use at most 320 MiB of HBM per device.

v0:
```python
import math
import jax
import jax.numpy as jnp
from jax import lax
from jax.sharding import PartitionSpec as P

epsilon = 1e-06
masked_score = -1e30


def with_halo(block, sides, width):
    for axis, dim in sides:
        count = lax.axis_size(axis)
        forward = [(i, i + 1) for i in range(count - 1)]
        backward = [(target, source) for source, target in forward]
        low = lax.ppermute(
            lax.slice_in_dim(block, block.shape[dim] - width, None, axis=dim), axis, forward
        )
        high = lax.ppermute(lax.slice_in_dim(block, 0, width, axis=dim), axis, backward)
        block = jnp.concatenate([low, block, high], axis=dim)
    return block


def select_size(size_table, position):
    marks = jnp.arange(size_table.shape[0], dtype=jnp.int32) == position
    return jnp.sum(jnp.where(marks, size_table, 0))


def lookup(size_table, positions):
    marks = positions[:, None] == jnp.arange(size_table.shape[0], dtype=jnp.int32)[None, :]
    return jnp.sum(jnp.where(marks, size_table[None, :], 0), axis=1)


def rms_scale(values_in, gain_vec):
    wide = values_in.astype(jnp.float32)
    return wide * lax.rsqrt(jnp.mean(wide * wide, axis=-1, keepdims=True) + epsilon) * gain_vec


def edge_rows(frames, row_count, col_count):
    height = frames.shape[1]
    breadth = frames.shape[2]
    last_row = lax.dynamic_slice_in_dim(frames, row_count - 1, 1, 1)
    frames = lax.dynamic_update_slice_in_dim(frames, last_row, height - 1, 1)
    last_col = lax.dynamic_slice_in_dim(frames, col_count - 1, 1, 2)
    return lax.dynamic_update_slice_in_dim(frames, last_col, breadth - 1, 2)


def settle(padded, row_count, col_count):
    bottom = padded[:, -1:]
    padded = lax.dynamic_update_slice_in_dim(padded, bottom, row_count + 1, 1)
    right_col = padded[:, :, -1:]
    return lax.dynamic_update_slice_in_dim(padded, right_col, col_count + 1, 2)


def convolve(extended, kernel):
    channels = extended.shape[3]
    height = extended.shape[1] - 2
    breadth = extended.shape[2] - 2
    columns = [
        extended[t_step, a_step : a_step + height, b_step : b_step + breadth]
        for t_step in range(3)
        for a_step in range(3)
        for b_step in range(3)
    ]
    stacked = jnp.concatenate(columns, axis=-1).reshape(height * breadth, 27 * channels)
    product = jnp.dot(
        stacked, kernel.reshape(27 * channels, kernel.shape[-1]), preferred_element_type=jnp.float32
    )
    return product.reshape(height, breadth, kernel.shape[-1])


def upsample(frames):
    return jnp.repeat(jnp.repeat(frames, 2, axis=1), 2, axis=2)


def local(
    tokens,
    row_sizes,
    col_sizes,
    norm_gain,
    query_weight,
    key_weight,
    value_weight,
    out_weight,
    cache_one,
    gain_one,
    conv_one,
    cache_two,
    gain_two,
    conv_two,
):
    tile_rows, tile_cols, channels = tokens.shape
    col_devices = lax.axis_size("col")
    row_count = select_size(row_sizes, lax.axis_index("row"))
    col_count = select_size(col_sizes, lax.axis_index("col"))
    per_device = tile_rows * tile_cols
    scale = 1.0 / math.sqrt(channels)
    flat_normed = rms_scale(tokens, norm_gain).astype(jnp.bfloat16).reshape(per_device, channels)
    queries = jnp.dot(flat_normed, query_weight, preferred_element_type=jnp.float32).astype(
        jnp.bfloat16
    )
    own_keys = jnp.dot(flat_normed, key_weight, preferred_element_type=jnp.float32).astype(
        jnp.bfloat16
    )
    own_values = jnp.dot(flat_normed, value_weight, preferred_element_type=jnp.float32).astype(
        jnp.bfloat16
    )
    key_rows = lax.all_gather(own_keys, ("row", "col"), axis=0, tiled=True)
    running_max = jnp.full((per_device,), masked_score, jnp.float32)
    slot_index = jnp.arange(key_rows.shape[0], dtype=jnp.int32)
    device = slot_index // per_device
    local_slot = slot_index - device * per_device
    tile_row = device // col_devices
    tile_col = device - tile_row * col_devices
    local_row = local_slot // tile_cols
    local_col = local_slot - local_row * tile_cols
    usable = (local_row < lookup(row_sizes, tile_row)) & (local_col < lookup(col_sizes, tile_col))
    scores = jnp.einsum("qc,kc->qk", queries, key_rows, preferred_element_type=jnp.float32) * scale
    scores = jnp.where(usable[None, :], scores, masked_score)
    new_max = jnp.maximum(running_max, jnp.max(scores, axis=1))
    expos = jnp.exp(scores - new_max[:, None]) * usable[None, :].astype(jnp.float32)
    denominator = jnp.sum(expos, axis=1)
    accumulated = jnp.dot(
        expos.astype(jnp.bfloat16),
        lax.all_gather(own_values, ("row", "col"), axis=0, tiled=True),
        preferred_element_type=jnp.float32,
    )
    attention = (accumulated / denominator[:, None]).astype(jnp.bfloat16)
    projected = jnp.dot(attention, out_weight, preferred_element_type=jnp.float32).reshape(
        tile_rows, tile_cols, channels
    )
    mixed = (tokens.astype(jnp.float32) + projected).astype(jnp.bfloat16)
    act_one = jax.nn.silu(rms_scale(mixed, gain_one)).astype(jnp.bfloat16)
    frames_one = jnp.concatenate([cache_one, act_one[None]], axis=0)
    prepared = edge_rows(frames_one, row_count, col_count)
    padded = with_halo(prepared, (("row", 1), ("col", 2)), 1)
    extended = settle(padded, row_count, col_count)
    y_one = convolve(extended, conv_one).astype(jnp.bfloat16)
    act_small = jax.nn.silu(rms_scale(y_one, gain_two)).astype(jnp.bfloat16)[None]
    fine_rows = 2 * row_count
    fine_cols = 2 * col_count
    frames_two = jnp.concatenate([cache_two, upsample(act_small)], axis=0)
    prepared_two = edge_rows(frames_two, fine_rows, fine_cols)
    padded_two = with_halo(prepared_two, (("row", 1), ("col", 2)), 1)
    extended_two = settle(padded_two, fine_rows, fine_cols)
    y_two = convolve(extended_two, conv_two)
    row_usable = jnp.arange(2 * tile_rows, dtype=jnp.int32) < fine_rows
    col_usable = jnp.arange(2 * tile_cols, dtype=jnp.int32) < fine_cols
    usable = (row_usable[:, None] & col_usable[None, :])[:, :, None]
    return jnp.where(usable, y_two, 0.0).astype(jnp.bfloat16)


def solution(mesh):
    placed = (
        P("row", "col", None),
        P(),
        P(),
        P(),
        P(),
        P(),
        P(),
        P(),
        P(None, "row", "col", None),
        P(),
        P(),
        P(None, "row", "col", None),
        P(),
        P(),
    )
    return jax.shard_map(
        local, mesh=mesh, in_specs=placed, out_specs=P("row", "col", None), check_vma=False
    )
```

profile of v0, /device:TPU:3, one launch (start us, length us, event | category | flops | bytes accessed | tf_op | source)
XLA Modules:
  0.0 391.6 jit_solution(13467160023956242634)
XLA Ops:
  8.8 1.9 fusion.15
  10.8 1.9 fusion.16
  21.8 86.2 %all-gather.5.cloned.1.call-done = bf16[128,260,384]{2,1,0:T(8,128)(2,1)} async-done(((bf16[1,260,384]{2,1,0:T(8,128)(2,1)}), bf16[128,260,384]{2,1,0:T(8,128)(2,1)}) %all-gather.5.cloned.1.call-update) | async-done | bytes 25559056 | tf_op jit(solution)/shard_map/all_gather | solution.py:108
  108.0 31.3 %reshape.388 = bf16[33280,384]{1,0:T(8,128)(2,1)} reshape(bf16[128,260,384]{2,1,0:T(8,128)(2,1)} %all-gather.5.cloned.1.call-done) | data formatting | bytes 51118080
  139.3 25.2 %fusion.99 = (f32[260]{0:T(512)S(1)}, f32[260,33280]{1,0:T(8,128)}) fusion(bf16[33280,384]{1,0:T(8,128)(2,1)} %reshape.388, bf16[260,384]{1,0:T(8,128)(2,1)S(1)} %reshape.383, bf16[384,384]{1,0:T(8,128)(2,1)S(1)} %copy-done, pred[33280]{0:T(1024)(128)(4,1)S(1)} %get-tuple-element.6), kind=kOutput, calls=%fused_computation.208 | convolution fusion | flops 6748085248 | bytes 60699152 | tf_op jit(solution)/shard_map/qc,kc->qk/dot_general | solution.py:118
  164.5 17.4 %fusion.1 = f32[260]{0:T(512)S(1)} fusion(f32[260,33280]{1,0:T(8,128)} %get-tuple-element.16, f32[33280]{0:T(1024)S(1)} %get-tuple-element.5, f32[260]{0:T(512)S(1)} %broadcast_maximum_fusion), kind=kLoop, calls=%fused_computation.3 | loop fusion | flops 25958140 | bytes 34746400 | tf_op jit(solution)/shard_map/reduce_sum | solution.py:122
  181.9 22.9 %all-gather.7.cloned.1.call-done = bf16[128,260,384]{2,1,0:T(8,128)(2,1)} async-done(((bf16[1,260,384]{2,1,0:T(8,128)(2,1)}), bf16[128,260,384]{2,1,0:T(8,128)(2,1)}) %all-gather.7.cloned.1.call-update) | async-done | bytes 25559056 | tf_op jit(solution)/shard_map/all_gather | solution.py:125
  204.8 31.2 %reshape.390 = bf16[33280,384]{1,0:T(8,128)(2,1)} reshape(bf16[128,260,384]{2,1,0:T(8,128)(2,1)} %all-gather.7.cloned.1.call-done) | data formatting | bytes 51118080
  236.0 22.0 %fusion.12 = bf16[260,384]{1,0:T(8,128)(2,1)S(1)} fusion(bf16[33280,384]{1,0:T(8,128)(2,1)} %reshape.390, f32[260,33280]{1,0:T(8,128)} %get-tuple-element.16, f32[33280]{0:T(1024)S(1)} %get-tuple-element.5, f32[260]{0:T(512)S(1)} %broadcast_maximum_fusion, f32[260]{0:T(512)S(1)} %fusion.1), kind=kOutput, calls=%fused_computation.19 | convolution fusion | flops 6671508480 | bytes 60505120 | tf_op jit(solution)/shard_map/dot_general | solution.py:123
  260.6 3.3 collective-permute-start
  263.9 1.9 collective-permute-start.1
  269.5 1.9 collective-permute-start.2
  271.4 5.7 %collective-permute-start.3 = (bf16[3,15,1,384]{3,2,1,0:T(2,128)(2,1)S(1)}, bf16[3,15,1,384]{3,2,1,0:T(2,128)(2,1)}, u32[]{:S(2)}, u32[]{:S(2)}) collective-permute-start(bf16[3,15,1,384]{3,2,1,0:T(2,128)(2,1)S(1)} %get-tuple-element.12), channel_id=1, source_target_pairs={{1,0},{2,1},{3,2},{4,3},{5,4},{6,5},{7,6},{8,7},{9,8},{10,9},{11,1... | collective-permute-start | bytes 103688 | tf_op jit(solution)/shard_map/ppermute | solution.py:19
  285.7 6.2 %multiply_reduce_fusion = (f32[13,20]{1,0:T(8,128)S(1)}, f32[13,20,384]{2,1,0:T(8,128)S(1)}) fusion(bf16[13,20,10368]{2,1,0:T(8,128)(2,1)S(1)} %fusion.57, bf16[10368,384,1]{1,0,2:T(8,128)(2,1)} %bitcast.243), kind=kOutput, calls=%fused_computation.100 | convolution fusion | flops 2070681344 | bytes 13754384 | tf_op jit(solution)/shard_map/dot_general | solution.py:66
  295.2 3.4 dynamic_update_slice.29
  298.7 3.0 collective-permute-start.4
  301.7 1.9 collective-permute-start.5
  303.6 3.9 %collective-permute-done.5 = bf16[3,1,40,384]{3,2,1,0:T(8,128)(2,1)S(1)} collective-permute-done((bf16[3,1,40,384]{3,2,1,0:T(8,128)(2,1)S(1)}, bf16[3,1,40,384]{3,2,1,0:T(8,128)(2,1)S(1)}, u32[]{:S(2)}, u32[]{:S(2)}) %collective-permute-start.5) | collective-permute-done | bytes 92192 | tf_op jit(solution)/shard_map/ppermute | solution.py:19
  309.7 5.5 %collective-permute-start.7 = (bf16[3,28,1,384]{3,2,1,0:T(2,128)(2,1)S(1)}, bf16[3,28,1,384]{3,2,1,0:T(2,128)(2,1)}, u32[]{:S(2)}, u32[]{:S(2)}) collective-permute-start(bf16[3,28,1,384]{3,2,1,0:T(2,128)(2,1)S(1)} %get-tuple-element.8), channel_id=1, source_target_pairs={{1,0},{2,1},{3,2},{4,3},{5,4},{6,5},{7,6},{8,7},{9,8},{10,9},{11,1... | collective-permute-start | bytes 193544 | tf_op jit(solution)/shard_map/ppermute | solution.py:19
  315.2 7.9 %copy.21 = bf16[3,3,3,384,192]{3,2,1,0,4:T(4,128)(2,1)} copy(bf16[3,3,3,384,192]{3,4,2,1,0:T(8,128)(2,1)} %param.27) | data formatting | bytes 7962624 | tf_op args[13]
  323.1 10.1 %reshape.392 = bf16[10368,192,1]{0,1,2:T(8,128)(2,1)} reshape(bf16[3,3,3,384,192]{3,2,1,0,4:T(4,128)(2,1)} %copy.21) | data formatting | bytes 7962624 | tf_op jit(solution)/shard_map/reshape | solution.py:67
  333.9 4.4 %pad_maximum_fusion = bf16[3,28,42,384]{3,2,1,0:T(8,128)(2,1)S(1)} fusion(bf16[3,28,1,384]{3,2,1,0:T(2,128)(2,1)} %collective-permute-done.7, bf16[3,1,40,384]{3,2,1,0:T(8,128)(2,1)S(1)} %collective-permute-done.5, bf16[3,26,40,384]{3,2,1,0:T(8,128)(2,1)} %copy-done.2, bf16[3,1,40,384]{3,2,1,0:T(8,128)(2,1)S(1)} %collective-permute-done.4, ...), kind=kLoop, calls=%fused_computation.8 | loop fusion | flops 13547520 | bytes 5419008 | tf_op jit(solution)/shard_map/concatenate | solution.py:20
  338.5 3.6 dynamic_update_slice.31
  373.6 11.2 %fusion.7 = bf16[26,40,192]{2,1,0:T(8,128)(2,1)} fusion(bf16[26,40,10368]{2,1,0:T(8,128)(2,1)} %fusion.17, bf16[10368,192,1]{0,1,2:T(8,128)(2,1)S(1)} %copy-done.4, pred[26,40]{1,0:T(8,128)(4,1)S(1)} %broadcast_and_fusion), kind=kOutput, calls=%fused_computation.12 | convolution fusion | flops 4140963840 | bytes 25947152 | tf_op jit(solution)/shard_map/dot_general | solution.py:66
  (133 shorter events, 57.3 us)
Async XLA Ops:
  6.5 132.8 %copy-start = (bf16[384,384]{1,0:T(8,128)(2,1)S(1)}, bf16[384,384]{1,0:T(8,128)(2,1)}, u32[]{:S(2)}) copy-start(bf16[384,384]{1,0:T(8,128)(2,1)} %param.18) | copy-start | bytes 884740
  6.5 101.5 %all-gather.5.cloned.1.call-start = ((), (), s32[]{:S(2)}) async-start(), calls=%async_computation | async-start | bytes 26155008 | tf_op jit(solution)/shard_map/all_gather | solution.py:108
  10.8 194.0 %all-gather.7.cloned.1.call-start = ((), (), s32[]{:S(2)}) async-start(), calls=%async_computation.1 | async-start | bytes 26155008 | tf_op jit(solution)/shard_map/all_gather | solution.py:125
  236.0 22.0 %copy-start.6 = (bf16[384,384]{1,0:T(8,128)(2,1)S(1)}, bf16[384,384]{1,0:T(8,128)(2,1)}, u32[]{:S(2)}) copy-start(bf16[384,384]{1,0:T(8,128)(2,1)} %param.21) | copy-start | bytes 884740
  236.0 22.4 %copy-start.5 = (bf16[13,20,384]{2,1,0:T(8,128)(2,1)S(1)}, bf16[13,20,384]{2,1,0:T(8,128)(2,1)}, u32[]{:S(2)}) copy-start(bf16[13,20,384]{2,1,0:T(8,128)(2,1)} %param.14) | copy-start | bytes 599044
  236.0 22.5 %copy-start.8 = (f32[384]{0:T(512)S(1)}, f32[384]{0:T(512)}, u32[]{:S(2)}) copy-start(f32[384]{0:T(512)} %param.23) | copy-start | bytes 4612
  260.6 19.6 %copy-start.3 = (bf16[3,13,20,384]{3,2,1,0:T(8,128)(2,1)}, bf16[3,13,20,384]{3,2,1,0:T(8,128)(2,1)S(1)}, u32[]{:S(2)}) copy-start(bf16[3,13,20,384]{3,2,1,0:T(8,128)(2,1)S(1)} %dynamic_update_slice.25) | copy-start | bytes 1797124
  260.6 7.5 %collective-permute-start = (bf16[3,1,20,384]{3,2,1,0:T(8,128)(2,1)S(1)}, bf16[3,1,20,384]{3,2,1,0:T(8,128)(2,1)S(1)}, u32[]{:S(2)}, u32[]{:S(2)}) collective-permute-start(bf16[3,1,20,384]{3,2,1,0:T(8,128)(2,1)S(1)} %get-tuple-element.13), channel_id=1, source_target_pairs={{0,16},{16,32},{32,48},{48,64},{64,80},{80,96},{96,112},{1,17},{17... | collective-permute-start | bytes 138248 | tf_op jit(solution)/shard_map/ppermute | solution.py:16
  263.9 5.5 %collective-permute-start.1 = (bf16[3,1,20,384]{3,2,1,0:T(8,128)(2,1)S(1)}, bf16[3,1,20,384]{3,2,1,0:T(8,128)(2,1)S(1)}, u32[]{:S(2)}, u32[]{:S(2)}) collective-permute-start(bf16[3,1,20,384]{3,2,1,0:T(8,128)(2,1)S(1)} %get-tuple-element.14), channel_id=1, source_target_pairs={{16,0},{32,16},{48,32},{64,48},{80,64},{96,80},{112,96},{17,1},{33... | collective-permute-start | bytes 138248 | tf_op jit(solution)/shard_map/ppermute | solution.py:19
  269.5 10.7 %collective-permute-start.2 = (bf16[3,15,1,384]{3,2,1,0:T(2,128)(2,1)S(1)}, bf16[3,15,1,384]{3,2,1,0:T(2,128)(2,1)S(1)}, u32[]{:S(2)}, u32[]{:S(2)}) collective-permute-start(bf16[3,15,1,384]{3,2,1,0:T(2,128)(2,1)S(1)} %get-tuple-element.11), channel_id=1, source_target_pairs={{0,1},{1,2},{2,3},{3,4},{4,5},{5,6},{6,7},{7,8},{8,9},{9,10},{10,1... | collective-permute-start | bytes 103688 | tf_op jit(solution)/shard_map/ppermute | solution.py:16
  271.4 8.8 %collective-permute-start.3 = (bf16[3,15,1,384]{3,2,1,0:T(2,128)(2,1)S(1)}, bf16[3,15,1,384]{3,2,1,0:T(2,128)(2,1)}, u32[]{:S(2)}, u32[]{:S(2)}) collective-permute-start(bf16[3,15,1,384]{3,2,1,0:T(2,128)(2,1)S(1)} %get-tuple-element.12), channel_id=1, source_target_pairs={{1,0},{2,1},{3,2},{4,3},{5,4},{6,5},{7,6},{8,7},{9,8},{10,9},{11,1... | collective-permute-start | bytes 103688 | tf_op jit(solution)/shard_map/ppermute | solution.py:19
  285.6 6.2 %copy-start.9 = (f32[384]{0:T(512)S(1)}, f32[384]{0:T(512)}, u32[]{:S(2)}) copy-start(f32[384]{0:T(512)} %param.26) | copy-start | bytes 4612
  298.7 34.5 %copy-start.2 = (bf16[3,26,40,384]{3,2,1,0:T(8,128)(2,1)}, bf16[3,26,40,384]{3,2,1,0:T(8,128)(2,1)S(1)}, u32[]{:S(2)}) copy-start(bf16[3,26,40,384]{3,2,1,0:T(8,128)(2,1)S(1)} %dynamic_update_slice.29) | copy-start | bytes 7188484
  298.7 4.9 %collective-permute-start.4 = (bf16[3,1,40,384]{3,2,1,0:T(8,128)(2,1)S(1)}, bf16[3,1,40,384]{3,2,1,0:T(8,128)(2,1)S(1)}, u32[]{:S(2)}, u32[]{:S(2)}) collective-permute-start(bf16[3,1,40,384]{3,2,1,0:T(8,128)(2,1)S(1)} %get-tuple-element.9), channel_id=1, source_target_pairs={{0,16},{16,32},{32,48},{48,64},{64,80},{80,96},{96,112},{1,17},{17... | collective-permute-start | bytes 276488 | tf_op jit(solution)/shard_map/ppermute | solution.py:16
  301.7 5.9 %collective-permute-start.5 = (bf16[3,1,40,384]{3,2,1,0:T(8,128)(2,1)S(1)}, bf16[3,1,40,384]{3,2,1,0:T(8,128)(2,1)S(1)}, u32[]{:S(2)}, u32[]{:S(2)}) collective-permute-start(bf16[3,1,40,384]{3,2,1,0:T(8,128)(2,1)S(1)} %get-tuple-element.10), channel_id=1, source_target_pairs={{16,0},{32,16},{48,32},{64,48},{80,64},{96,80},{112,96},{17,1},{33... | collective-permute-start | bytes 276488 | tf_op jit(solution)/shard_map/ppermute | solution.py:19
  307.7 25.5 %collective-permute-start.6 = (bf16[3,28,1,384]{3,2,1,0:T(2,128)(2,1)S(1)}, bf16[3,28,1,384]{3,2,1,0:T(2,128)(2,1)S(1)}, u32[]{:S(2)}, u32[]{:S(2)}) collective-permute-start(bf16[3,28,1,384]{3,2,1,0:T(2,128)(2,1)S(1)} %get-tuple-element.7), channel_id=1, source_target_pairs={{0,1},{1,2},{2,3},{3,4},{4,5},{5,6},{6,7},{7,8},{8,9},{9,10},{10,1... | collective-permute-start | bytes 193544 | tf_op jit(solution)/shard_map/ppermute | solution.py:16
  309.7 24.2 %collective-permute-start.7 = (bf16[3,28,1,384]{3,2,1,0:T(2,128)(2,1)S(1)}, bf16[3,28,1,384]{3,2,1,0:T(2,128)(2,1)}, u32[]{:S(2)}, u32[]{:S(2)}) collective-permute-start(bf16[3,28,1,384]{3,2,1,0:T(2,128)(2,1)S(1)} %get-tuple-element.8), channel_id=1, source_target_pairs={{1,0},{2,1},{3,2},{4,3},{5,4},{6,5},{7,6},{8,7},{9,8},{10,9},{11,1... | collective-permute-start | bytes 193544 | tf_op jit(solution)/shard_map/ppermute | solution.py:19
  333.2 0.7 copy-start.7
  364.0 9.6 %copy-start.4 = (bf16[10368,192,1]{0,1,2:T(8,128)(2,1)S(1)}, bf16[10368,192,1]{0,1,2:T(8,128)(2,1)}, u32[]{:S(2)}) copy-start(bf16[10368,192,1]{0,1,2:T(8,128)(2,1)} %reshape.392) | copy-start | bytes 11943940
  373.6 11.2 %copy-start.1 = (bf16[384,384]{1,0:T(8,128)(2,1)S(1)}, bf16[384,384]{1,0:T(8,128)(2,1)}, u32[]{:S(2)}) copy-start(bf16[384,384]{1,0:T(8,128)(2,1)} %param.18) | copy-start | bytes 884740
Sparse Core Ops, SparseCore 0:
  10.9 97.1 all-gather.4
  111.0 93.7 all-gather.6
where the time goes:
time: 394 us; the launch traced here: 392 us
  local copies, waits for them, and re-layouts  131 us (33%)
  waiting for transfers between devices  114 us (29%)
  matrix products  68.7 us (17%)
  other arithmetic  32.2 us (8%)
  starting transfers between devices  25.1 us (6%)
  between operations  20.4 us (5%)
    unnamed x77, local copies, waits for them, and re-layouts  106 us
    all_gather x1, waiting for transfers between devices, local(): key_rows = lax.all_gather(own_keys, ('row', 'col'), axis=0, tiled=True)  86.2 us
    dot_general x1, matrix products, local(): jnp.einsum('qc,kc->qk', queries, key_rows, preferred_element_type=jnp.flo...  25.2 us
    all_gather x1, waiting for transfers between devices, local(): lax.all_gather(own_values, ('row', 'col'), axis=0, tiled=True)  22.9 us
    dot_general x1, matrix products, local(): jnp.dot(expos.astype(jnp.bfloat16), lax.all_gather(own_values, ('row', 'c...  22 us
    reduce_sum x1, other arithmetic, local(): denominator = jnp.sum(expos, axis=1)  17.4 us
    dot_general x2, matrix products, convolve(): jnp.dot(stacked, kernel.reshape(27 * channels, kernel.shape[-1]), preferr...  17.3 us
    ppermute x4, starting transfers between devices, with_halo(): lax.ppermute(lax.slice_in_dim(block, 0, width, axis=dim), axis, backward)  15 us
  transfers between devices with their start and end apart: 10, of which 4 were waited for; matrix products, arithmetic and copies ran while one was open for 26% of the time, Pallas kernels for 0%

commit v1 on v0

--- a/solution.py
+++ b/solution.py
@@ -120,9 +120,13 @@
     new_max = jnp.maximum(running_max, jnp.max(scores, axis=1))
     expos = jnp.exp(scores - new_max[:, None]) * usable[None, :].astype(jnp.float32)
     denominator = jnp.sum(expos, axis=1)
+    positions_scan = lambda buf, link_axis, dim_at: jnp.concatenate(
+        lax.all_to_all(jnp.stack([buf for _ in range(lax.axis_size(link_axis))]), link_axis, 0, 0),
+        axis=dim_at,
+    )
     accumulated = jnp.dot(
         expos.astype(jnp.bfloat16),
-        lax.all_gather(own_values, ("row", "col"), axis=0, tiled=True),
+        positions_scan(own_values, ("row", "col"), 0),
         preferred_element_type=jnp.float32,
     )
     attention = (accumulated / denominator[:, None]).astype(jnp.bfloat16)

time: 394 us -> 711 us (1.80)
  waiting for transfers between devices: 114 us -> 395 us
  starting transfers between devices: 25.1 us -> 55.6 us
  local copies, waits for them, and re-layouts: 131 us -> 139 us
    all_to_all x0 -> x1, waiting for transfers between devices: none -> 390 us  [local(): lax.all_to_all(jnp.stack([buf for _ in range(lax.axis_size(link_axis))]),...]
    all_gather x1, waiting for transfers between devices: 86.2 us -> 0.01 us  [local(): key_rows = lax.all_gather(own_keys, ('row', 'col'), axis=0, tiled=True)]
    unnamed x77 -> x82, local copies, waits for them, and re-layouts: 106 us -> 73.5 us
    reshape x0 -> x1, local copies, waits for them, and re-layouts: none -> 31.2 us  [local(): jnp.concatenate(lax.all_to_all(jnp.stack([buf for _ in range(lax.axis_siz...]
    all_gather x1 -> x0, waiting for transfers between devices: 22.9 us -> none  [local(): lax.all_gather(own_values, ('row', 'col'), axis=0, tiled=True)]
    ppermute x4, starting transfers between devices: 10 us -> 32.9 us  [with_halo(): lax.ppermute(lax.slice_in_dim(block, block.shape[dim] - width, None, axis...]
    all_to_all x0 -> x1, starting transfers between devices: none -> 11.2 us  [local(): lax.all_to_all(jnp.stack([buf for _ in range(lax.axis_size(link_axis))]),...]
    another operation x0 -> x1, local copies, waits for them, and re-layouts: none -> 8.76 us  [local(): jnp.stack([buf for _ in range(lax.axis_size(link_axis))])]
  transfers between devices with their start and end apart: 10 -> 10, of which waited for: 4 -> 3; matrix products, arithmetic and copies ran while one was open for 26% -> 9% of each run, Pallas kernels for 0% -> 0%
where the time goes in v1:
time: 711 us; the launch traced here: 705 us
  waiting for transfers between devices  395 us (56%)
  local copies, waits for them, and re-layouts  139 us (20%)
  matrix products  67.5 us (9%)
  starting transfers between devices  55.6 us (8%)
  other arithmetic  27.4 us (4%)
  between operations  20.6 us (3%)
    all_to_all x1, waiting for transfers between devices, local(): lax.all_to_all(jnp.stack([buf for _ in range(lax.axis_size(link_axis))]),...  390 us
    unnamed x82, local copies, waits for them, and re-layouts  73.5 us
    ppermute x4, starting transfers between devices, with_halo(): lax.ppermute(lax.slice_in_dim(block, block.shape[dim] - width, None, axis...  32.9 us
    reshape x1, local copies, waits for them, and re-layouts, local(): jnp.concatenate(lax.all_to_all(jnp.stack([buf for _ in range(lax.axis_siz...  31.2 us
    dot_general x1, matrix products, local(): jnp.einsum('qc,kc->qk', queries, key_rows, preferred_element_type=jnp.flo...  24.6 us
    dot_general x1, matrix products, local(): jnp.dot(expos.astype(jnp.bfloat16), positions_scan(own_values, ('row', 'c...  22 us
    dot_general x2, matrix products, convolve(): jnp.dot(stacked, kernel.reshape(27 * channels, kernel.shape[-1]), preferr...  17.3 us
    reduce_sum x1, other arithmetic, local(): denominator = jnp.sum(expos, axis=1)  15.2 us
  transfers between devices with their start and end apart: 10, of which 3 were waited for; matrix products, arithmetic and copies ran while one was open for 9% of the time, Pallas kernels for 0%

profile of v1, /device:TPU:3, one launch (start us, length us, event | category | flops | bytes accessed | tf_op | source)
XLA Modules:
  0.0 704.7 jit_solution(5974541317709002844)
XLA Ops:
  8.8 1.9 fusion.15
  12.0 8.8 %stack.2 = bf16[128,260,384]{2,1,0:T(8,128)(2,1)} broadcast(bf16[260,384]{1,0:T(8,128)(2,1)S(1)} %convolution_convert_fusion.1), dimensions={1,2} | broadcast | bytes 25758720 | tf_op jit(solution)/shard_map/stack | solution.py:124
  20.8 11.2 %all-to-all-start = ((bf16[128,260,384]{2,1,0:T(8,128)(2,1)}), bf16[128,260,384]{2,1,0:T(8,128)(2,1)}, u32[]{:S(2)}, u32[]{:S(2)}) async-start(bf16[128,260,384]{2,1,0:T(8,128)(2,1)} %stack.2), calls=%async_computation | async-start | bytes 51904512 | tf_op jit(solution)/shard_map/all_to_all | solution.py:124
  37.5 389.8 %all-to-all-done = bf16[128,260,384]{2,1,0:T(8,128)(2,1)} async-done(((bf16[128,260,384]{2,1,0:T(8,128)(2,1)}), bf16[128,260,384]{2,1,0:T(8,128)(2,1)}, u32[]{:S(2)}, u32[]{:S(2)}) %all-to-all-start) | async-done | bytes 25559072 | tf_op jit(solution)/shard_map/all_to_all | solution.py:124
  427.3 31.2 %reshape.389 = bf16[33280,384]{1,0:T(8,128)(2,1)} reshape(bf16[128,260,384]{2,1,0:T(8,128)(2,1)} %all-to-all-done) | data formatting | bytes 51118080 | tf_op jit(solution)/shard_map/reshape | solution.py:123
  458.6 31.2 %reshape.394 = bf16[33280,384]{1,0:T(8,128)(2,1)} reshape(bf16[128,260,384]{2,1,0:T(8,128)(2,1)} %all-gather.3.cloned.1.call-done) | data formatting | bytes 51118080
  489.8 24.6 %fusion.98 = (f32[260]{0:T(512)S(1)}, f32[260,33280]{1,0:T(8,128)}) fusion(bf16[33280,384]{1,0:T(8,128)(2,1)} %reshape.394, bf16[260,384]{1,0:T(8,128)(2,1)S(1)} %reshape.388, bf16[384,384]{1,0:T(8,128)(2,1)S(1)} %copy-done, pred[33280]{0:T(1024)(128)(4,1)S(1)} %get-tuple-element.6), kind=kOutput, calls=%fused_computation.207 | convolution fusion | flops 6748085248 | bytes 60699152 | tf_op jit(solution)/shard_map/qc,kc->qk/dot_general | solution.py:118
  514.4 15.2 %fusion.1 = f32[260]{0:T(512)S(1)} fusion(f32[260,33280]{1,0:T(8,128)} %get-tuple-element.16, f32[33280]{0:T(1024)S(1)} %get-tuple-element.5, f32[260]{0:T(512)S(1)} %broadcast_maximum_fusion), kind=kLoop, calls=%fused_computation.3 | loop fusion | flops 25958140 | bytes 34746400 | tf_op jit(solution)/shard_map/reduce_sum | solution.py:122
  529.6 22.0 %fusion.12 = bf16[260,384]{1,0:T(8,128)(2,1)S(1)} fusion(bf16[33280,384]{1,0:T(8,128)(2,1)} %reshape.389, f32[260,33280]{1,0:T(8,128)} %get-tuple-element.16, f32[33280]{0:T(1024)S(1)} %get-tuple-element.5, f32[260]{0:T(512)S(1)} %broadcast_maximum_fusion, f32[260]{0:T(512)S(1)} %fusion.1), kind=kOutput, calls=%fused_computation.19 | convolution fusion | flops 6671508480 | bytes 60505120 | tf_op jit(solution)/shard_map/dot_general | solution.py:127
  554.2 22.3 %collective-permute-start = (bf16[3,1,20,384]{3,2,1,0:T(8,128)(2,1)S(1)}, bf16[3,1,20,384]{3,2,1,0:T(8,128)(2,1)S(1)}, u32[]{:S(2)}, u32[]{:S(2)}) collective-permute-start(bf16[3,1,20,384]{3,2,1,0:T(8,128)(2,1)S(1)} %get-tuple-element.13), channel_id=1, source_target_pairs={{0,16},{16,32},{32,48},{48,64},{64,80},{80,96},{96,112},{1,17},{17... | collective-permute-start | bytes 138248 | tf_op jit(solution)/shard_map/ppermute | solution.py:16
  576.6 2.1 collective-permute-start.1
  582.2 1.9 collective-permute-start.2
  584.1 5.5 collective-permute-start.3
  598.3 6.2 multiply_reduce_fusion
  607.8 3.4 dynamic_update_slice.29
  611.3 3.1 collective-permute-start.4
  616.4 3.9 collective-permute-done.5
  620.5 5.6 collective-permute-start.6
  626.1 1.9 collective-permute-start.7
  628.1 7.9 %copy.21 = bf16[3,3,3,384,192]{3,2,1,0,4:T(4,128)(2,1)} copy(bf16[3,3,3,384,192]{3,4,2,1,0:T(8,128)(2,1)} %param.27) | data formatting | bytes 7962624 | tf_op args[13]
  635.9 10.1 %reshape.396 = bf16[10368,192,1]{0,1,2:T(8,128)(2,1)} reshape(bf16[3,3,3,384,192]{3,2,1,0,4:T(4,128)(2,1)} %copy.21) | data formatting | bytes 7962624 | tf_op jit(solution)/shard_map/reshape | solution.py:67
  646.7 4.4 pad_maximum_fusion
  651.3 3.6 dynamic_update_slice.31
  686.7 11.2 %fusion.7 = bf16[26,40,192]{2,1,0:T(8,128)(2,1)} fusion(bf16[26,40,10368]{2,1,0:T(8,128)(2,1)} %fusion.16, bf16[10368,192,1]{0,1,2:T(8,128)(2,1)S(1)} %copy-done.4, pred[26,40]{1,0:T(8,128)(4,1)S(1)} %broadcast_and_fusion), kind=kOutput, calls=%fused_computation.12 | convolution fusion | flops 4140963840 | bytes 25947152 | tf_op jit(solution)/shard_map/dot_general | solution.py:66
  (139 shorter events, 55.1 us)
Async XLA Ops:
  6.5 483.2 %copy-start = (bf16[384,384]{1,0:T(8,128)(2,1)S(1)}, bf16[384,384]{1,0:T(8,128)(2,1)}, u32[]{:S(2)}) copy-start(bf16[384,384]{1,0:T(8,128)(2,1)} %param.18) | copy-start | bytes 884740
  6.5 452.0 %all-gather.3.cloned.1.call-start = ((), (), s32[]{:S(2)}) async-start(), calls=%async_computation.1 | async-start | bytes 26155008 | tf_op jit(solution)/shard_map/all_gather | solution.py:108
  20.8 11.3 %copy-start.6 = (bf16[2,13,20,384]{3,0,2,1:T(2,128)(2,1)S(1)}, bf16[2,13,20,384]{3,0,2,1:T(2,128)(2,1)}, u32[]{:S(2)}) copy-start(bf16[2,13,20,384]{3,0,2,1:T(2,128)(2,1)} %param.22) | copy-start | bytes 1198084
  20.8 11.3 %copy-start.11 = (s32[8]{0:T(128)S(1)}, s32[8]{0:T(128)}, u32[]{:S(2)}) copy-start(s32[8]{0:T(128)} %param.15) | copy-start | bytes 100
  20.8 13.4 %copy-start.12 = (s32[16]{0:T(128)S(1)}, s32[16]{0:T(128)}, u32[]{:S(2)}) copy-start(s32[16]{0:T(128)} %param.16) | copy-start | bytes 196
  20.8 406.5 %all-to-all-start = ((bf16[128,260,384]{2,1,0:T(8,128)(2,1)}), bf16[128,260,384]{2,1,0:T(8,128)(2,1)}, u32[]{:S(2)}, u32[]{:S(2)}) async-start(bf16[128,260,384]{2,1,0:T(8,128)(2,1)} %stack.2), calls=%async_computation | async-start | bytes 51904512 | tf_op jit(solution)/shard_map/all_to_all | solution.py:124
  529.6 22.1 %copy-start.7 = (bf16[384,384]{1,0:T(8,128)(2,1)S(1)}, bf16[384,384]{1,0:T(8,128)(2,1)}, u32[]{:S(2)}) copy-start(bf16[384,384]{1,0:T(8,128)(2,1)} %param.21) | copy-start | bytes 884740
  529.6 22.4 %copy-start.5 = (bf16[13,20,384]{2,1,0:T(8,128)(2,1)S(1)}, bf16[13,20,384]{2,1,0:T(8,128)(2,1)}, u32[]{:S(2)}) copy-start(bf16[13,20,384]{2,1,0:T(8,128)(2,1)} %param.14) | copy-start | bytes 599044
  529.6 22.6 %copy-start.9 = (f32[384]{0:T(512)S(1)}, f32[384]{0:T(512)}, u32[]{:S(2)}) copy-start(f32[384]{0:T(512)} %param.23) | copy-start | bytes 4612
  554.2 38.6 %copy-start.3 = (bf16[3,13,20,384]{3,2,1,0:T(8,128)(2,1)}, bf16[3,13,20,384]{3,2,1,0:T(8,128)(2,1)S(1)}, u32[]{:S(2)}) copy-start(bf16[3,13,20,384]{3,2,1,0:T(8,128)(2,1)S(1)} %dynamic_update_slice.25) | copy-start | bytes 1797124
  554.2 26.7 %collective-permute-start = (bf16[3,1,20,384]{3,2,1,0:T(8,128)(2,1)S(1)}, bf16[3,1,20,384]{3,2,1,0:T(8,128)(2,1)S(1)}, u32[]{:S(2)}, u32[]{:S(2)}) collective-permute-start(bf16[3,1,20,384]{3,2,1,0:T(8,128)(2,1)S(1)} %get-tuple-element.13), channel_id=1, source_target_pairs={{0,16},{16,32},{32,48},{48,64},{64,80},{80,96},{96,112},{1,17},{17... | collective-permute-start | bytes 138248 | tf_op jit(solution)/shard_map/ppermute | solution.py:16
  576.6 5.5 collective-permute-start.1
  582.2 10.7 %collective-permute-start.2 = (bf16[3,15,1,384]{3,2,1,0:T(2,128)(2,1)S(1)}, bf16[3,15,1,384]{3,2,1,0:T(2,128)(2,1)S(1)}, u32[]{:S(2)}, u32[]{:S(2)}) collective-permute-start(bf16[3,15,1,384]{3,2,1,0:T(2,128)(2,1)S(1)} %get-tuple-element.11), channel_id=1, source_target_pairs={{0,1},{1,2},{2,3},{3,4},{4,5},{5,6},{6,7},{7,8},{8,9},{9,10},{10,1... | collective-permute-start | bytes 103688 | tf_op jit(solution)/shard_map/ppermute | solution.py:16
  584.1 8.7 %collective-permute-start.3 = (bf16[3,15,1,384]{3,2,1,0:T(2,128)(2,1)S(1)}, bf16[3,15,1,384]{3,2,1,0:T(2,128)(2,1)}, u32[]{:S(2)}, u32[]{:S(2)}) collective-permute-start(bf16[3,15,1,384]{3,2,1,0:T(2,128)(2,1)S(1)} %get-tuple-element.12), channel_id=1, source_target_pairs={{1,0},{2,1},{3,2},{4,3},{5,4},{6,5},{7,6},{8,7},{9,8},{10,9},{11,1... | collective-permute-start | bytes 103688 | tf_op jit(solution)/shard_map/ppermute | solution.py:19
  598.3 6.2 copy-start.10
  611.3 34.8 %copy-start.2 = (bf16[3,26,40,384]{3,2,1,0:T(8,128)(2,1)}, bf16[3,26,40,384]{3,2,1,0:T(8,128)(2,1)S(1)}, u32[]{:S(2)}) copy-start(bf16[3,26,40,384]{3,2,1,0:T(8,128)(2,1)S(1)} %dynamic_update_slice.29) | copy-start | bytes 7188484
  611.3 5.1 collective-permute-start.4
  614.4 5.9 collective-permute-start.5
  620.5 25.5 %collective-permute-start.6 = (bf16[3,28,1,384]{3,2,1,0:T(2,128)(2,1)S(1)}, bf16[3,28,1,384]{3,2,1,0:T(2,128)(2,1)S(1)}, u32[]{:S(2)}, u32[]{:S(2)}) collective-permute-start(bf16[3,28,1,384]{3,2,1,0:T(2,128)(2,1)S(1)} %get-tuple-element.7), channel_id=1, source_target_pairs={{0,1},{1,2},{2,3},{3,4},{4,5},{5,6},{6,7},{7,8},{8,9},{9,10},{10,1... | collective-permute-start | bytes 193544 | tf_op jit(solution)/shard_map/ppermute | solution.py:16
  626.1 20.6 %collective-permute-start.7 = (bf16[3,28,1,384]{3,2,1,0:T(2,128)(2,1)S(1)}, bf16[3,28,1,384]{3,2,1,0:T(2,128)(2,1)}, u32[]{:S(2)}, u32[]{:S(2)}) collective-permute-start(bf16[3,28,1,384]{3,2,1,0:T(2,128)(2,1)S(1)} %get-tuple-element.8), channel_id=1, source_target_pairs={{1,0},{2,1},{3,2},{4,3},{5,4},{6,5},{7,6},{8,7},{9,8},{10,9},{11,1... | collective-permute-start | bytes 193544 | tf_op jit(solution)/shard_map/ppermute | solution.py:19
  646.0 0.7 copy-start.8
  677.3 9.4 %copy-start.4 = (bf16[10368,192,1]{0,1,2:T(8,128)(2,1)S(1)}, bf16[10368,192,1]{0,1,2:T(8,128)(2,1)}, u32[]{:S(2)}) copy-start(bf16[10368,192,1]{0,1,2:T(8,128)(2,1)} %reshape.396) | copy-start | bytes 11943940
  686.7 11.2 %copy-start.1 = (bf16[384,384]{1,0:T(8,128)(2,1)S(1)}, bf16[384,384]{1,0:T(8,128)(2,1)}, u32[]{:S(2)}) copy-start(bf16[384,384]{1,0:T(8,128)(2,1)} %param.18) | copy-start | bytes 884740
Sparse Core Ops, SparseCore 0:
  10.9 366.1 all-gather.2
